TPU v7x, 512 devices: a whole 4x4x16 slice. The times are simulated.
512 devices in a mesh: row: 16 (over z), col: 32 (over y, x, core).
Axes of the slice: x: 4, y: 4, z: 16, core: 2. Of those that a mesh axis runs over, the one named last changes fastest.
Arguments:
- flow_state: bfloat16 [131072, 256], P(('col', 'row')), may hold values from -6 to 6
- link_state: bfloat16 [65536, 256], P(('row', 'col')), may hold values from -6 to 6
- incidence: bfloat16 [16, 32, 24, 128, 128], P('row', 'col'), may hold values from -0.29882812 to 0.29882812
- tile_flow: int32 [16, 32, 24], P('row', 'col'), may hold values from 0 to 31
- tile_link: int32 [16, 32, 24], P('row', 'col'), may hold values from 0 to 31
- tile_live: int32 [16, 32, 24], P('row', 'col'), may hold values from 0 to 1, as said below
- link_gain: float32 [256], replicated, may hold values from 0.5 to 2
- link_agg_weight: bfloat16 [256, 256], replicated, may hold values from -0.375 to 0.375
- link_self_weight: bfloat16 [256, 256], replicated, may hold values from -0.375 to 0.375
- link_out_weight: bfloat16 [256, 256], replicated, may hold values from -0.375 to 0.375
- flow_gain: float32 [256], replicated, may hold values from 0.5 to 2
- flow_agg_weight: bfloat16 [256, 256], replicated, may hold values from -0.375 to 0.375
- flow_self_weight: bfloat16 [256, 256], replicated, may hold values from -0.375 to 0.375
- flow_out_weight: bfloat16 [256, 256], replicated, may hold values from -0.375 to 0.375
Outputs:
- link_next: bfloat16 [65536, 256], P(('row', 'col'))
- flow_next: bfloat16 [131072, 256], P(('col', 'row'))
Inputs may be any that keep to these rules, and one draw needn't show every extreme that they name: `tile_live`: in every draw some group pair has all 24 slots live; the number of live slots differs from pair to pair.
All inputs are finite; a program needn't handle non-finite values.
Results may differ from a plain program's by a relative error of at most 0.018.
Values may be sent and summed in bfloat16 or wider, within the bound.
No kernel may reach another device: no remote copies, remote signals or barrier semaphores. Data moves between devices by JAX's collectives and lax.ppermute only.
A program may use at most 64 MiB of HBM per device.

v0:
```python
import jax
import jax.numpy as jnp
from jax import lax
from jax.sharding import PartitionSpec as P

H = 256
BS = 128


def state_update(totals, state, gain, agg_weight, self_weight, out_weight):
    scale = lax.rsqrt(jnp.mean(totals * totals, axis=-1, keepdims=True) + 1e-05)
    normed = (totals * scale * gain).astype(jnp.bfloat16)
    before = jnp.dot(normed, agg_weight, preferred_element_type=jnp.float32) + jnp.dot(
        state, self_weight, preferred_element_type=jnp.float32
    )
    hidden = jax.nn.silu(before).astype(jnp.bfloat16)
    return (
        state.astype(jnp.float32) + jnp.dot(hidden, out_weight, preferred_element_type=jnp.float32)
    ).astype(jnp.bfloat16)


def selector(targets, live_slots, block_count):
    select = (targets[None, :] == jnp.arange(block_count, dtype=jnp.int32)[:, None]).astype(
        jnp.float32
    )
    return select * live_slots.astype(jnp.float32)[None, :]


def on_device(
    flow_state,
    link_state,
    incidence,
    tile_flow,
    tile_link,
    tile_live,
    link_gain,
    link_agg_weight,
    link_self_weight,
    link_out_weight,
    flow_gain,
    flow_agg_weight,
    flow_self_weight,
    flow_out_weight,
):
    coefs = incidence[0, 0]
    flow_slots = tile_flow[0, 0]
    link_slots = tile_link[0, 0]
    live_slots = tile_live[0, 0]
    slot_count = coefs.shape[0]
    flow_blocks_here = flow_state.shape[0] // BS
    link_blocks_here = link_state.shape[0] // BS
    link_blocks = link_blocks_here * lax.axis_size("col")
    flow_group = lax.all_gather(flow_state, "row", axis=0, tiled=True)
    flow_blocks = flow_group.shape[0] // BS
    flow_pieces = jnp.take(flow_group.reshape(flow_blocks, BS, H), flow_slots, axis=0)
    link_terms = jnp.einsum(
        "tij,tih->tjh", coefs, flow_pieces, preferred_element_type=jnp.float32
    ).reshape(slot_count, BS * H)
    link_select = selector(link_slots, live_slots, link_blocks)
    chosen = link_select
    link_sum = lax.psum_scatter(
        jnp.dot(chosen, link_terms, precision=lax.Precision.HIGHEST).astype(jnp.bfloat16),
        "col",
        scatter_dimension=0,
        tiled=True,
    ).astype(jnp.float32)
    link_next = state_update(
        link_sum.reshape(link_blocks_here * BS, H),
        link_state,
        link_gain,
        link_agg_weight,
        link_self_weight,
        link_out_weight,
    )
    link_group = lax.all_gather(link_next, "col", axis=0, tiled=True)
    link_pieces = jnp.take(link_group.reshape(link_blocks, BS, H), link_slots, axis=0)
    flow_terms = jnp.einsum(
        "tij,tjh->tih", coefs, link_pieces, preferred_element_type=jnp.float32
    ).reshape(slot_count, BS * H)
    flow_select = selector(flow_slots, live_slots, flow_blocks)
    chosen = flow_select
    flow_sum = lax.psum_scatter(
        jnp.dot(chosen, flow_terms, precision=lax.Precision.HIGHEST).astype(jnp.bfloat16),
        "row",
        scatter_dimension=0,
        tiled=True,
    ).astype(jnp.float32)
    flow_next = state_update(
        flow_sum.reshape(flow_blocks_here * BS, H),
        flow_state,
        flow_gain,
        flow_agg_weight,
        flow_self_weight,
        flow_out_weight,
    )
    return (link_next, flow_next)


def solution(mesh):
    return jax.shard_map(
        on_device,
        mesh=mesh,
        in_specs=(
            P(("col", "row"), None),
            P(("row", "col"), None),
            P("row", "col", None, None, None),
            P("row", "col", None),
            P("row", "col", None),
            P("row", "col", None),
            P(),
            P(),
            P(),
            P(),
            P(),
            P(),
            P(),
            P(),
        ),
        out_specs=(P(("row", "col"), None), P(("col", "row"), None)),
        check_vma=False,
    )
```

profile of v0, /device:TPU:2, one launch (start us, length us, event | category | flops | bytes accessed | tf_op | source)
XLA Modules:
  0.0 468.4 jit_solution(17944627231696059716)
XLA Ops:
  7.2 0.7 all-gather.3.cloned.1.call-update
  8.0 0.7 compare_select_fusion.1
  8.6 0.7 compare_and_fusion.1
  9.3 0.7 convert_bitcast_fusion
  9.9 77.7 %all-gather.3.cloned.1.call-done = bf16[4096,256]{1,0:T(8,128)(2,1)} async-done(((bf16[256,256]{1,0:T(8,128)(2,1)}), bf16[4096,256]{1,0:T(8,128)(2,1)}) %all-gather.3.cloned.1.call-update) | async-done | bytes 2097168 | tf_op jit(solution)/shard_map/all_gather | solution.py:53
  87.7 2.2 gather_fusion
  89.9 2.4 convolution_bitcast_fusion.1
  92.3 3.6 copy.26
  95.9 6.7 %convolution_convert_fusion.1 = bf16[32,32768]{1,0:T(8,128)(2,1)} fusion(f32[24,32768]{1,0:T(8,128)} %bitcast.40, f32[24]{0:T(128)S(1)} %convert_bitcast_fusion, s32[24]{0:T(128)S(1)} %bitcast.45), kind=kOutput, calls=%fused_computation.3 | convolution fusion | flops 303040000 | bytes 5243072 | tf_op jit(solution)/shard_map/dot_general | solution.py:62
  102.6 1.4 dynamic-slice
  104.0 133.2 %all-reduce.5.cloned.1.call-done = bf16[32,32768]{1,0:T(8,128)(2,1)} async-done(((bf16[32,32768]{1,0:T(8,128)(2,1)}), bf16[32,32768]{1,0:T(8,128)(2,1)}) %all-reduce.5.cloned.1.call-update) | async-done | bytes 2097168
  237.2 2.1 fusion.11
  239.7 0.9 fusion.5
  240.8 59.3 %all-gather.5.cloned.1.call-done = bf16[4096,256]{1,0:T(8,128)(2,1)} async-done(((bf16[128,256]{1,0:T(8,128)(2,1)}), bf16[4096,256]{1,0:T(8,128)(2,1)}) %all-gather.5.cloned.1.call-update) | async-done | bytes 2097168 | tf_op jit(solution)/shard_map/all_gather | solution.py:75
  300.1 2.2 gather_fusion.1
  302.3 2.4 convolution_bitcast_fusion
  304.7 3.6 copy.27
  308.3 6.7 %convolution_convert_fusion = bf16[32,32768]{1,0:T(8,128)(2,1)} fusion(f32[24,32768]{1,0:T(8,128)} %bitcast.39, s32[24]{0:T(128)S(1)} %bitcast.46, f32[24]{0:T(128)S(1)} %convert_bitcast_fusion), kind=kOutput, calls=%fused_computation.2 | convolution fusion | flops 303040000 | bytes 5243072 | tf_op jit(solution)/shard_map/dot_general | solution.py:83
  315.0 1.4 dynamic-slice.2
  317.0 142.1 %all-reduce.7.cloned.1.call-done = bf16[32,32768]{1,0:T(8,128)(2,1)} async-done(((bf16[32,32768]{1,0:T(8,128)(2,1)}), bf16[32,32768]{1,0:T(8,128)(2,1)}) %all-reduce.7.cloned.1.call-update) | async-done | bytes 2097168
  459.0 1.1 dynamic-slice_convert_fusion
  460.2 0.2 reshape.70
  460.6 0.2 fusion.10
  460.8 1.0 fusion.4
  (43 shorter events, 0.8 us)
Async XLA Ops:
  7.2 82.8 %copy-start = (bf16[1,1,24,128,128]{4,3,2,1,0:T(8,128)(2,1)S(1)}, bf16[1,1,24,128,128]{4,3,2,1,0:T(8,128)(2,1)}, u32[]{:S(2)}) copy-start(bf16[1,1,24,128,128]{4,3,2,1,0:T(8,128)(2,1)} %param.18) | copy-start | bytes 2359300
  7.2 80.5 %all-gather.3.cloned.1.call-start = ((), (), s32[]{:S(2)}) async-start(), calls=%async_computation | async-start | bytes 2228224 | tf_op jit(solution)/shard_map/all_gather | solution.py:53
  7.9 229.3 %all-reduce.5.cloned.1.call-start = ((), (), s32[]{:S(2)}) async-start(), calls=%async_computation.2 | async-start | bytes 4194304
  92.3 3.6 copy-start.6
  102.5 136.9 %copy-start.2 = (bf16[256,256]{1,0:T(8,128)(2,1)S(1)}, bf16[256,256]{1,0:T(8,128)(2,1)}, u32[]{:S(2)}) copy-start(bf16[256,256]{1,0:T(8,128)(2,1)} %param.23) | copy-start | bytes 393220
  102.5 137.0 %copy-start.4 = (f32[256]{0:T(256)S(1)}, f32[256]{0:T(256)}, u32[]{:S(2)}) copy-start(f32[256]{0:T(256)} %param.22) | copy-start | bytes 3076
  102.5 137.2 %copy-start.8 = (bf16[256,256]{1,0:T(8,128)(2,1)S(1)}, bf16[256,256]{1,0:T(8,128)(2,1)}, u32[]{:S(2)}) copy-start(bf16[256,256]{1,0:T(8,128)(2,1)} %param.25) | copy-start | bytes 393220
  102.5 137.2 %copy-start.9 = (bf16[256,256]{1,0:T(8,128)(2,1)S(1)}, bf16[256,256]{1,0:T(8,128)(2,1)}, u32[]{:S(2)}) copy-start(bf16[256,256]{1,0:T(8,128)(2,1)} %param.24) | copy-start | bytes 393220
  102.5 137.2 %copy-start.12 = (bf16[128,256]{1,0:T(8,128)(2,1)S(1)}, bf16[128,256]{1,0:T(8,128)(2,1)}, u32[]{:S(2)}) copy-start(bf16[128,256]{1,0:T(8,128)(2,1)} %param.17) | copy-start | bytes 196612
  102.6 197.5 %all-gather.5.cloned.1.call-start = ((), (), s32[]{:S(2)}) async-start(), calls=%async_computation.1 | async-start | bytes 2162688 | tf_op jit(solution)/shard_map/all_gather | solution.py:75
  240.7 218.3 %all-reduce.7.cloned.1.call-start = ((), (), s32[]{:S(2)}) async-start(), calls=%async_computation.3 | async-start | bytes 4194304
  304.7 3.6 copy-start.7
  314.9 145.6 %copy-start.1 = (bf16[256,256]{1,0:T(8,128)(2,1)S(1)}, bf16[256,256]{1,0:T(8,128)(2,1)}, u32[]{:S(2)}) copy-start(bf16[256,256]{1,0:T(8,128)(2,1)} %param.27) | copy-start | bytes 393220
  314.9 145.6 %copy-start.5 = (f32[256]{0:T(256)S(1)}, f32[256]{0:T(256)}, u32[]{:S(2)}) copy-start(f32[256]{0:T(256)} %param.26) | copy-start | bytes 3076
  314.9 145.9 %copy-start.3 = (bf16[256,256]{1,0:T(8,128)(2,1)S(1)}, bf16[256,256]{1,0:T(8,128)(2,1)}, u32[]{:S(2)}) copy-start(bf16[256,256]{1,0:T(8,128)(2,1)} %param.16) | copy-start | bytes 393220
  314.9 145.9 %copy-start.10 = (bf16[256,256]{1,0:T(8,128)(2,1)S(1)}, bf16[256,256]{1,0:T(8,128)(2,1)}, u32[]{:S(2)}) copy-start(bf16[256,256]{1,0:T(8,128)(2,1)} %param.29) | copy-start | bytes 393220
  314.9 145.9 %copy-start.11 = (bf16[256,256]{1,0:T(8,128)(2,1)S(1)}, bf16[256,256]{1,0:T(8,128)(2,1)}, u32[]{:S(2)}) copy-start(bf16[256,256]{1,0:T(8,128)(2,1)} %param.28) | copy-start | bytes 393220
Sparse Core Ops, SparseCore 0:
  10.1 77.5 all-gather.2
  102.7 134.4 all-reduce.4
  240.9 59.1 all-gather.4
  315.1 143.8 all-reduce.6
where the time goes:
time: 469 us; the launch traced here: 468 us
  waiting for transfers between devices  413 us (88%)
  matrix products  20.5 us (4%)
  local copies, waits for them, and re-layouts  14.7 us (3%)
  between operations  14.6 us (3%)
  other arithmetic  5.46 us (1%)
    unnamed x6, waiting for transfers between devices  276 us
    all_gather x1, waiting for transfers between devices, on_device(): flow_group = lax.all_gather(flow_state, 'row', axis=0, tiled=True)  77.7 us
    all_gather x1, waiting for transfers between devices, on_device(): link_group = lax.all_gather(link_next, 'col', axis=0, tiled=True)  59.3 us
    unnamed x30, local copies, waits for them, and re-layouts  9.94 us
  transfers between devices with their start and end apart: 4, of which 4 were waited for; matrix products, arithmetic and copies ran while one was open for 1% of the time, Pallas kernels for 0%

commit v1 on v0

--- a/solution.py
+++ b/solution.py
@@ -50,7 +50,9 @@
     flow_blocks_here = flow_state.shape[0] // BS
     link_blocks_here = link_state.shape[0] // BS
     link_blocks = link_blocks_here * lax.axis_size("col")
-    flow_group = lax.all_gather(flow_state, "row", axis=0, tiled=True)
+    flow_group = jnp.concatenate(
+        lax.all_to_all(jnp.stack([flow_state] * lax.axis_size("row")), "row", 0, 0), axis=0
+    )
     flow_blocks = flow_group.shape[0] // BS
     flow_pieces = jnp.take(flow_group.reshape(flow_blocks, BS, H), flow_slots, axis=0)
     link_terms = jnp.einsum(

time: 469 us -> 502 us (1.070)
  waiting for transfers between devices: 413 us -> 430 us
  starting transfers between devices: 0.16 us -> 15.6 us
    all_to_all x0 -> x1, waiting for transfers between devices: none -> 95.5 us  [on_device(): lax.all_to_all(jnp.stack([flow_state] * lax.axis_size('row')), 'row', 0, 0)]
    all_gather x1 -> x0, waiting for transfers between devices: 77.7 us -> none  [on_device(): flow_group = lax.all_gather(flow_state, 'row', axis=0, tiled=True)]
    all_to_all x0 -> x1, starting transfers between devices: none -> 15.3 us  [on_device(): lax.all_to_all(jnp.stack([flow_state] * lax.axis_size('row')), 'row', 0, 0)]
    unnamed x6 -> x5, waiting for transfers between devices: 276 us -> 275 us
where the time goes in v1:
time: 502 us
  waiting for transfers between devices  430 us (86%)
  matrix products  21.8 us (4%)
  local copies, waits for them, and re-layouts  16.8 us (3%)
  starting transfers between devices  15.6 us (3%)
  between operations  14.7 us (3%)
    unnamed x5, waiting for transfers between devices  275 us
    all_to_all x1, waiting for transfers between devices, on_device(): lax.all_to_all(jnp.stack([flow_state] * lax.axis_size('row')), 'row', 0, 0)  95.5 us
    all_gather x1, waiting for transfers between devices, on_device(): link_group = lax.all_gather(link_next, 'col', axis=0, tiled=True)  59.1 us
    all_to_all x1, starting transfers between devices, on_device(): lax.all_to_all(jnp.stack([flow_state] * lax.axis_size('row')), 'row', 0, 0)  15.3 us
  transfers between devices with their start and end apart: 4, of which 4 were waited for; matrix products, arithmetic and copies ran while one was open for 1% of the time, Pallas kernels for 0%

profile of v1, /device:TPU:2, one launch (start us, length us, event | category | flops | bytes accessed | tf_op | source)
XLA Modules:
  0.0 501.9 jit_solution(2158927677295947725)
XLA Ops:
  7.2 2.5 stack.2
  9.7 15.3 %all-to-all-start = ((bf16[16,256,256]{2,1,0:T(8,128)(2,1)}), bf16[16,256,256]{2,1,0:T(8,128)(2,1)S(1)}, u32[]{:S(2)}, u32[]{:S(2)}) async-start(bf16[16,256,256]{2,1,0:T(8,128)(2,1)} %stack.2), calls=%async_computation | async-start | bytes 4194304 | tf_op jit(solution)/shard_map/all_to_all | solution.py:54
  25.2 95.5 %all-to-all-done = bf16[16,256,256]{2,1,0:T(8,128)(2,1)S(1)} async-done(((bf16[16,256,256]{2,1,0:T(8,128)(2,1)}), bf16[16,256,256]{2,1,0:T(8,128)(2,1)S(1)}, u32[]{:S(2)}, u32[]{:S(2)}) %all-to-all-start) | async-done | bytes 2097184 | tf_op jit(solution)/shard_map/all_to_all | solution.py:54
  120.6 1.9 gather_fusion
  122.5 3.7 convolution_bitcast_fusion.1
  126.2 3.6 copy.26
  129.8 6.7 %convolution_convert_fusion.1 = bf16[32,32768]{1,0:T(8,128)(2,1)} fusion(f32[24,32768]{1,0:T(8,128)} %bitcast.40, f32[24]{0:T(128)S(1)} %convert_bitcast_fusion, s32[24]{0:T(128)S(1)} %bitcast.45), kind=kOutput, calls=%fused_computation.3 | convolution fusion | flops 303040000 | bytes 5243072 | tf_op jit(solution)/shard_map/dot_general | solution.py:64
  136.6 1.4 dynamic-slice
  138.0 132.7 %all-reduce.5.cloned.1.call-done = bf16[32,32768]{1,0:T(8,128)(2,1)} async-done(((bf16[32,32768]{1,0:T(8,128)(2,1)}), bf16[32,32768]{1,0:T(8,128)(2,1)}) %all-reduce.5.cloned.1.call-update) | async-done | bytes 2097168
  270.7 2.1 fusion.11
  273.0 0.2 fusion.15
  273.2 0.9 fusion.5
  274.2 0.2 all-reduce.7.cloned.1.call-start
  274.4 59.1 %all-gather.2.cloned.1.call-done = bf16[4096,256]{1,0:T(8,128)(2,1)} async-done(((bf16[128,256]{1,0:T(8,128)(2,1)}), bf16[4096,256]{1,0:T(8,128)(2,1)}) %all-gather.2.cloned.1.call-update) | async-done | bytes 2097168 | tf_op jit(solution)/shard_map/all_gather | solution.py:77
  333.6 2.2 gather_fusion.1
  335.8 2.4 convolution_bitcast_fusion
  338.2 3.6 copy.27
  341.7 6.7 %convolution_convert_fusion = bf16[32,32768]{1,0:T(8,128)(2,1)} fusion(f32[24,32768]{1,0:T(8,128)} %bitcast.39, s32[24]{0:T(128)S(1)} %bitcast.46, f32[24]{0:T(128)S(1)} %convert_bitcast_fusion), kind=kOutput, calls=%fused_computation.2 | convolution fusion | flops 303040000 | bytes 5243072 | tf_op jit(solution)/shard_map/dot_general | solution.py:85
  348.4 1.4 dynamic-slice.2
  350.4 142.1 %all-reduce.7.cloned.1.call-done = bf16[32,32768]{1,0:T(8,128)(2,1)} async-done(((bf16[32,32768]{1,0:T(8,128)(2,1)}), bf16[32,32768]{1,0:T(8,128)(2,1)}) %all-reduce.7.cloned.1.call-update) | async-done | bytes 2097168
  492.6 1.1 dynamic-slice_convert_fusion
  493.7 0.2 reshape.68
  494.1 0.2 fusion.10
  494.4 1.0 fusion.4
  (45 shorter events, 0.5 us)
Async XLA Ops:
  7.2 115.3 %copy-start = (bf16[1,1,24,128,128]{4,3,2,1,0:T(8,128)(2,1)S(1)}, bf16[1,1,24,128,128]{4,3,2,1,0:T(8,128)(2,1)}, u32[]{:S(2)}) copy-start(bf16[1,1,24,128,128]{4,3,2,1,0:T(8,128)(2,1)} %param.18) | copy-start | bytes 2359300
  9.7 15.4 %copy-start.7 = (s32[1,1,24]{2,1,0:T(1,128)S(1)}, s32[1,1,24]{2,1,0:T(1,128)}, u32[]{:S(2)}) copy-start(s32[1,1,24]{2,1,0:T(1,128)} %param.19) | copy-start | bytes 292
  9.7 15.4 %copy-start.13 = (s32[1,1,24]{2,1,0:T(1,128)S(1)}, s32[1,1,24]{2,1,0:T(1,128)}, u32[]{:S(2)}) copy-start(s32[1,1,24]{2,1,0:T(1,128)} %param.21) | copy-start | bytes 292
  9.7 110.9 %all-to-all-start = ((bf16[16,256,256]{2,1,0:T(8,128)(2,1)}), bf16[16,256,256]{2,1,0:T(8,128)(2,1)S(1)}, u32[]{:S(2)}, u32[]{:S(2)}) async-start(bf16[16,256,256]{2,1,0:T(8,128)(2,1)} %stack.2), calls=%async_computation | async-start | bytes 4194304 | tf_op jit(solution)/shard_map/all_to_all | solution.py:54
  25.0 245.7 %all-reduce.5.cloned.1.call-start = ((), (), s32[]{:S(2)}) async-start(), calls=%async_computation.2 | async-start | bytes 4194304
  126.2 3.6 copy-start.6
  136.5 136.5 %copy-start.3 = (bf16[256,256]{1,0:T(8,128)(2,1)S(1)}, bf16[256,256]{1,0:T(8,128)(2,1)}, u32[]{:S(2)}) copy-start(bf16[256,256]{1,0:T(8,128)(2,1)} %param.23) | copy-start | bytes 393220
  136.5 136.5 %copy-start.4 = (f32[256]{0:T(256)S(1)}, f32[256]{0:T(256)}, u32[]{:S(2)}) copy-start(f32[256]{0:T(256)} %param.22) | copy-start | bytes 3076
  136.5 136.7 %copy-start.8 = (bf16[256,256]{1,0:T(8,128)(2,1)S(1)}, bf16[256,256]{1,0:T(8,128)(2,1)}, u32[]{:S(2)}) copy-start(bf16[256,256]{1,0:T(8,128)(2,1)} %param.25) | copy-start | bytes 393220
  136.5 136.7 %copy-start.9 = (bf16[256,256]{1,0:T(8,128)(2,1)S(1)}, bf16[256,256]{1,0:T(8,128)(2,1)}, u32[]{:S(2)}) copy-start(bf16[256,256]{1,0:T(8,128)(2,1)} %param.24) | copy-start | bytes 393220
  136.5 136.7 %copy-start.12 = (bf16[128,256]{1,0:T(8,128)(2,1)S(1)}, bf16[128,256]{1,0:T(8,128)(2,1)}, u32[]{:S(2)}) copy-start(bf16[128,256]{1,0:T(8,128)(2,1)} %param.17) | copy-start | bytes 196612
  136.5 197.0 %all-gather.2.cloned.1.call-start = ((), (), s32[]{:S(2)}) async-start(), calls=%async_computation.1 | async-start | bytes 2162688 | tf_op jit(solution)/shard_map/all_gather | solution.py:77
  274.2 218.4 %all-reduce.7.cloned.1.call-start = ((), (), s32[]{:S(2)}) async-start(), calls=%async_computation.3 | async-start | bytes 4194304
  348.4 145.7 %copy-start.1 = (bf16[256,256]{1,0:T(8,128)(2,1)S(1)}, bf16[256,256]{1,0:T(8,128)(2,1)}, u32[]{:S(2)}) copy-start(bf16[256,256]{1,0:T(8,128)(2,1)} %param.27) | copy-start | bytes 393220
  348.4 145.7 %copy-start.5 = (f32[256]{0:T(256)S(1)}, f32[256]{0:T(256)}, u32[]{:S(2)}) copy-start(f32[256]{0:T(256)} %param.26) | copy-start | bytes 3076
  348.4 146.0 %copy-start.2 = (bf16[256,256]{1,0:T(8,128)(2,1)S(1)}, bf16[256,256]{1,0:T(8,128)(2,1)}, u32[]{:S(2)}) copy-start(bf16[256,256]{1,0:T(8,128)(2,1)} %param.16) | copy-start | bytes 393220
  348.4 146.0 %copy-start.10 = (bf16[256,256]{1,0:T(8,128)(2,1)S(1)}, bf16[256,256]{1,0:T(8,128)(2,1)}, u32[]{:S(2)}) copy-start(bf16[256,256]{1,0:T(8,128)(2,1)} %param.29) | copy-start | bytes 393220
  348.4 146.0 %copy-start.11 = (bf16[256,256]{1,0:T(8,128)(2,1)S(1)}, bf16[256,256]{1,0:T(8,128)(2,1)}, u32[]{:S(2)}) copy-start(bf16[256,256]{1,0:T(8,128)(2,1)} %param.28) | copy-start | bytes 393220
Sparse Core Ops, SparseCore 0:
  136.6 134.0 all-reduce.4
  274.4 59.1 all-gather.1
  348.5 143.9 all-reduce.6
